TPU v7x, 32 devices: a whole 2x2x4 slice. The times are simulated.
32 devices in a mesh: row: 4 (over z), col: 8 (over y, x, core).
Axes of the slice: x: 2, y: 2, z: 4, core: 2. Of those that a mesh axis runs over, the one named last changes fastest.
Arguments:
- a_trail: float32 [16384, 16384], P('row', 'col'), may hold values from -60 to 60, as said below
- a_panel: float32 [16384, 256], P(('row', 'col')), may hold values from -6 to 6
- l_panel: float32 [16384, 256], P(('row', 'col')), may hold values from -0.5 to 0.5
- a_diag: float32 [256, 256], replicated, may hold values from -60 to 60, as said below
- l_inverse: float32 [256, 256], replicated, may hold values from -4 to 4, as said below
Outputs:
- trail_out: float32 [16384, 16384], P('row', 'col')
- panel_out: float32 [16384, 256], P(('row', 'col'))
Inputs may be any that keep to these rules, and one draw needn't show every extreme that they name: `a_trail`: symmetric. `a_diag`: symmetric. `l_inverse`: lower triangular with a positive diagonal.
All inputs are finite; a program needn't handle non-finite values.
Results may differ from a plain program's by a relative error of at most 0.0003.
Values sent between devices are 32-bit elements; how exact they have to be, the bound alone decides.
A program may use at most 192 MiB of HBM per device.

v0:
```python
import functools

import jax
import jax.numpy as jnp
from jax import lax
from jax.experimental import pallas as pl
from jax.experimental.layout import Layout, with_layout_constraint
from jax.experimental.pallas import tpu as pltpu
from jax.sharding import PartitionSpec as P

NS_STEPS = 8
BOTH = ("row", "col")
MESH_ID = pl.DeviceIdType.MESH


def product(left, right):
    return jnp.dot(left, right, precision=lax.Precision.HIGHEST, preferred_element_type=jnp.float32)


def large_product(left, right):
    return jnp.dot(left, right, precision=lax.Precision.HIGH, preferred_element_type=jnp.float32)


def newton_inverse(matrix):
    identity = jnp.eye(matrix.shape[0], dtype=jnp.float32)
    approx = identity
    for _ in range(NS_STEPS):
        approx = product(approx, 2.0 * identity - product(matrix, approx))
    return approx


def right_solve(factor, values):
    return lax.linalg.triangular_solve(
        factor, values, left_side=False, lower=True, transpose_a=True
    )


def greet_all(rows, cols):
    count = rows * cols
    me = lax.axis_index("row") * cols + lax.axis_index("col")
    barrier = pltpu.get_barrier_semaphore()

    def greet(step, carry):
        at = lax.rem(me + step, count)
        pl.semaphore_signal(
            barrier, inc=1, device_id=(at // cols, lax.rem(at, cols)), device_id_type=MESH_ID
        )
        return carry

    lax.fori_loop(1, count, greet, 0)
    pl.semaphore_wait(barrier, count - 1)


def sum_steps(rows, cols, x_ref, o_ref, recv, red, send_a, recv_a, send_b, recv_b, held):
    count = rows * cols
    me = lax.axis_index("row") * cols + lax.axis_index("col")

    def peer(step):
        at = lax.rem(me + step, count)
        return at, (at // cols, lax.rem(at, cols))

    def owner(at):
        return (at * x_ref.shape[1]) // held

    def scatter(step):
        at, device = peer(step)
        return pltpu.make_async_remote_copy(
            src_ref=x_ref.at[at], dst_ref=recv.at[step], send_sem=send_a.at[step],
            recv_sem=recv_a.at[step], device_id=device, device_id_type=MESH_ID,
        )

    def gather(step):
        device = peer(step)[1]
        return pltpu.make_async_remote_copy(
            src_ref=red, dst_ref=o_ref.at[me], send_sem=send_b.at[step],
            recv_sem=recv_b.at[step], device_id=device, device_id_type=MESH_ID,
        )

    def loop(action):
        def body(step, carry):
            action(step)
            return carry

        lax.fori_loop(1, count, body, 0)

    def sends(step, action):
        if held is None:
            action()
        else:
            pl.when(owner(peer(step)[0]) == me)(action)

    def first():
        loop(lambda step: sends(step, lambda: scatter(step).start()))

    def second():
        if held is None:
            def add(step, total):
                scatter(step).wait_recv()
                return total + recv[step]

            total = lax.fori_loop(1, count, add, x_ref[me])
            red[...] = total
            o_ref[me] = total
        else:
            source = owner(me)

            @pl.when(source == me)
            def _():
                red[...] = x_ref[me]
                o_ref[me] = x_ref[me]

            @pl.when(source != me)
            def _():
                step = lax.rem(me + count - source, count)
                scatter(step).wait_recv()
                red[...] = recv[step]
                o_ref[me] = recv[step]
        loop(lambda step: gather(step).start())

    def third():
        def finish(step):
            gather(step).wait_recv()
            sends(step, lambda: scatter(step).wait_send())
            gather(step).wait_send()

        loop(finish)

    return first, second, third


def sum_scratch(count, piece, width):
    return [
        pltpu.VMEM((count, piece, width), jnp.float32),
        pltpu.VMEM((piece, width), jnp.float32),
        pltpu.SemaphoreType.DMA((count,)),
        pltpu.SemaphoreType.DMA((count,)),
        pltpu.SemaphoreType.DMA((count,)),
        pltpu.SemaphoreType.DMA((count,)),
    ]


def sum_kernel(rows, cols, *refs):
    first, second, third = sum_steps(rows, cols, *refs, None)
    greet_all(rows, cols)
    first()
    second()
    third()


def first_kernel(rows, cols, held, x_ref, a_ref, o_ref, a_first, recv, red, send_a, recv_a,
                 send_b, recv_b, send_p, recv_p, own_sem):
    i = lax.axis_index("row")
    c = lax.axis_index("col")
    height, width = a_first.shape
    first, second, third = sum_steps(
        rows, cols, x_ref, o_ref, recv, red, send_a, recv_a, send_b, recv_b, held
    )

    def piece(to):
        return pltpu.make_async_remote_copy(
            src_ref=a_ref.at[pl.ds(to * height, height), pl.ds(0, width)], dst_ref=a_first,
            send_sem=send_p.at[to], recv_sem=recv_p.at[0], device_id=(i, to),
            device_id_type=MESH_ID,
        )

    own = pltpu.make_async_copy(
        a_ref.at[pl.ds(0, height), pl.ds(0, width)], a_first, own_sem.at[0]
    )
    greet_all(rows, cols)
    first()

    @pl.when(c == 0)
    def _():
        own.start()
        for to in range(1, cols):
            piece(to).start()

    second()
    third()

    @pl.when(c == 0)
    def _():
        own.wait()
        for to in range(1, cols):
            piece(to).wait_send()

    @pl.when(c != 0)
    def _():
        piece(1).wait_recv()


def sum_all(rows, cols, value, ident):
    count = rows * cols
    height, width = value.shape
    piece = height // count
    spec = pl.BlockSpec(memory_space=pltpu.VMEM)
    out = pl.pallas_call(
        functools.partial(sum_kernel, rows, cols),
        out_shape=jax.ShapeDtypeStruct((count, piece, width), jnp.float32),
        in_specs=[spec],
        out_specs=spec,
        scratch_shapes=sum_scratch(count, piece, width),
        compiler_params=pltpu.CompilerParams(collective_id=ident, has_side_effects=True),
    )(value.reshape(count, piece, width))
    return out.reshape(height, width)


def first_exchange(rows, cols, value, held, a_trail, height, block_width, ident):
    count = rows * cols
    tall, width = value.shape
    piece = tall // count
    spec = pl.BlockSpec(memory_space=pltpu.VMEM)
    anywhere = pl.BlockSpec(memory_space=pl.ANY)
    out, a_first = pl.pallas_call(
        functools.partial(first_kernel, rows, cols, held),
        out_shape=(
            jax.ShapeDtypeStruct((count, piece, width), jnp.float32),
            jax.ShapeDtypeStruct((height, block_width), jnp.float32),
        ),
        in_specs=[spec, anywhere],
        out_specs=(spec, spec),
        scratch_shapes=sum_scratch(count, piece, width) + [
            pltpu.SemaphoreType.DMA((cols,)),
            pltpu.SemaphoreType.DMA((1,)),
            pltpu.SemaphoreType.DMA((1,)),
        ],
        compiler_params=pltpu.CompilerParams(collective_id=ident, has_side_effects=True),
    )(value.reshape(count, piece, width), a_trail)
    return out.reshape(tall, width), a_first


def gather_kernel(rows, cols, p_ref, x_ref, v_ref, o_ref, x_rows, v_rows, x_cols, recv, red,
                  send_a, recv_a, send_b, recv_b, col_send, col_recv, row_send, row_recv,
                  twin_send, twin_recv, own_sem):
    chips = cols // 2
    i = lax.axis_index("row")
    c = lax.axis_index("col")
    me = i * cols + c
    core = lax.rem(c, 2)
    twin = c + 1 - 2 * core
    first, second, third = sum_steps(
        rows, cols, p_ref, o_ref, recv, red, send_a, recv_a, send_b, recv_b, None
    )
    greet_all(rows, cols)
    first()

    block = me // rows
    slot = lax.rem(me, rows)
    own = [
        pltpu.make_async_copy(x_ref, x_rows.at[c], own_sem.at[0]),
        pltpu.make_async_copy(v_ref, v_rows.at[c], own_sem.at[1]),
    ]
    own_col = pltpu.make_async_copy(x_ref, x_cols.at[slot], own_sem.at[2])

    def to_col(step):
        return pltpu.make_async_remote_copy(
            src_ref=x_ref, dst_ref=x_cols.at[slot], send_sem=col_send.at[step],
            recv_sem=col_recv.at[slot], device_id=(lax.rem(i + step, rows), block),
            device_id_type=MESH_ID,
        )

    def from_col(k):
        return pltpu.make_async_remote_copy(
            src_ref=x_ref, dst_ref=x_cols.at[k], send_sem=col_send.at[0],
            recv_sem=col_recv.at[k], device_id=(i, twin), device_id_type=MESH_ID,
        )

    pieces = ((x_ref, x_rows), (v_ref, v_rows))

    def to_row(which, step):
        src, dst = pieces[which]
        return pltpu.make_async_remote_copy(
            src_ref=src, dst_ref=dst.at[c], send_sem=row_send.at[which, step],
            recv_sem=row_recv.at[which, step],
            device_id=(i, lax.rem(c + 2 * step, cols)), device_id_type=MESH_ID,
        )

    def to_twin(which, step):
        src, dst = pieces[which]
        at = lax.rem(c + cols - 2 * step, cols)
        return pltpu.make_async_remote_copy(
            src_ref=dst.at[at] if step else src, dst_ref=dst.at[at],
            send_sem=twin_send.at[which, step], recv_sem=twin_recv.at[which, step],
            device_id=(i, twin), device_id_type=MESH_ID,
        )

    is_own = block == c
    for step in range(1, rows):
        to_col(step).start()

    @pl.when(is_own)
    def _():
        own_col.start()

    @pl.when(jnp.logical_not(is_own))
    def _():
        to_col(0).start()

    for which in range(2):
        for step in range(1, chips):
            to_row(which, step).start()
    for which in range(2):
        own[which].start()
        to_twin(which, 0).start()
    second()
    for which in range(2):
        for step in range(1, chips):
            to_row(which, step).wait_recv()
            to_twin(which, step).start()
    for which in range(2):
        for step in range(chips):
            to_twin(which, step).wait_recv()
    for k in range(rows):
        source_is_me = c * rows + k == me

        @pl.when(source_is_me)
        def _():
            own_col.wait()

        @pl.when(jnp.logical_not(source_is_me))
        def _(k=k):
            from_col(k).wait_recv()

    for which in range(2):
        own[which].wait()
        for step in range(chips):
            to_twin(which, step).wait_send()
            if step:
                to_row(which, step).wait_send()
    third()
    for step in range(1, rows):
        to_col(step).wait_send()

    @pl.when(jnp.logical_not(is_own))
    def _():
        to_col(0).wait_send()


def gather_both(rows, cols, part, x, v, ident):
    height, width = x.shape
    chips = cols // 2
    count = rows * cols
    piece = width // count
    near = pl.BlockSpec(memory_space=pltpu.VMEM)
    spec = pl.BlockSpec(memory_space=pl.ANY)
    tall = jax.ShapeDtypeStruct((cols, height, width), jnp.float32)
    total, x_rows, v_rows, x_cols = pl.pallas_call(
        functools.partial(gather_kernel, rows, cols),
        out_shape=(
            jax.ShapeDtypeStruct((count, piece, width), jnp.float32), tall, tall,
            jax.ShapeDtypeStruct((rows, height, width), jnp.float32),
        ),
        in_specs=[near, spec, spec],
        out_specs=(near, spec, spec, spec),
        scratch_shapes=sum_scratch(count, piece, width) + [
            pltpu.SemaphoreType.DMA((rows,)),
            pltpu.SemaphoreType.DMA((rows,)),
            pltpu.SemaphoreType.DMA((2, chips)),
            pltpu.SemaphoreType.DMA((2, chips)),
            pltpu.SemaphoreType.DMA((2, chips)),
            pltpu.SemaphoreType.DMA((2, chips)),
            pltpu.SemaphoreType.DMA((3,)),
        ],
        compiler_params=pltpu.CompilerParams(collective_id=ident, has_side_effects=True),
    )(part.reshape(count, piece, width), x, v)
    return (
        total.reshape(width, width), x_rows.reshape(-1, width), v_rows.reshape(-1, width), x_cols.reshape(-1, width)
    )


def shards(rows, cols, a_trail, a_panel, l_panel, a_diag, l_inverse):
    chips = cols // 2
    height = a_panel.shape[0]
    block_width = a_diag.shape[0]
    row_index = lax.axis_index("row")
    col_index = lax.axis_index("col")
    chip = col_index // 2
    core = col_index % 2
    me = row_index * cols + col_index
    sibling = [(c, c ^ 1) for c in range(cols)]

    def chip_shift(step):
        return [(c, (c + 2 * step) % cols) for c in range(cols)]

    def rows_from(shard):
        out = jnp.zeros((cols,) + shard.shape, jnp.float32)
        for step in range(chips):
            part = lax.ppermute(shard, "col", chip_shift(step)) if step else shard
            twin = lax.ppermute(part, "col", sibling)
            at = (col_index + cols - 2 * step) % cols
            out = lax.dynamic_update_index_in_dim(out, part, at, 0)
            out = lax.dynamic_update_index_in_dim(out, twin, at ^ 1, 0)
        return out.reshape(cols * shard.shape[0], shard.shape[1])

    def cols_from(shard):
        out = jnp.zeros((rows,) + shard.shape, jnp.float32)
        for step in range(rows):
            pairs = [
                (c * rows + (i + step) % rows, i * cols + c)
                for i in range(rows) for c in range(cols)
            ]
            part = lax.ppermute(shard, BOTH, pairs)
            out = lax.dynamic_update_index_in_dim(out, part, (row_index + step) % rows, 0)
        return out.reshape(rows * shard.shape[0], shard.shape[1])

    def sum_to_shard(values):
        parts = values.reshape(chips, 2, height, values.shape[1])

        def pick(to_chip, to_core):
            return lax.dynamic_slice(
                parts, (to_chip, to_core, 0, 0), (1, 1) + parts.shape[2:]
            ).reshape(parts.shape[2:])

        total = None
        for step in range(chips):
            to_chip = (chip + step) % chips
            both = pick(to_chip, core) + lax.ppermute(pick(to_chip, 1 - core), "col", sibling)
            if step:
                both = lax.ppermute(both, "col", chip_shift(step))
            total = both if total is None else total + both
        return total

    a11_new = product(product(l_inverse, a_diag), l_inverse.T)
    solved = product(a_panel, l_inverse.T)
    half_term = 0.5 * product(l_panel, a11_new)
    first_y = solved - half_term
    panel_out = first_y - half_term
    pair = jnp.concatenate((first_y, l_panel), axis=1)
    tall = min(height, block_width)
    first_pair, a_first = first_exchange(
        rows, cols, jnp.concatenate([pair[:tall]] * (block_width // tall), axis=0), tall,
        a_trail, height, block_width, 0,
    )
    first_swap = jnp.concatenate(
        (first_pair[:, block_width:], first_pair[:, :block_width]), axis=1
    )
    panel = a_first - product(pair, first_swap.T)
    global_rows = me * height + lax.iota(jnp.int32, height)
    next_panel = jnp.where((global_rows >= block_width)[:, None], panel, 0.0)
    picker = (
        global_rows[:, None] - block_width == lax.iota(jnp.int32, block_width)[None, :]
    ).astype(jnp.float32)
    stats = sum_all(
        rows, cols,
        jnp.concatenate(
            (product(next_panel.T, next_panel), product(picker.T, next_panel)), axis=1
        ),
        1,
    )
    late_pair, stats = lax.optimization_barrier((pair, stats))
    late_pair = with_layout_constraint(late_pair, Layout(major_to_minor=(0, 1)))
    factor = jnp.linalg.cholesky(stats[:, :block_width])
    solved_rows = right_solve(
        factor, jnp.concatenate((next_panel, stats[:, block_width:]), axis=0)
    )
    identity = jnp.eye(block_width, dtype=jnp.float32)
    g_inverse = newton_inverse(identity + solved_rows[height:]).T
    refl = solved_rows[:height] + picker

    pair_rows = rows_from(late_pair)
    pair_cols = cols_from(late_pair)
    swap_cols = jnp.concatenate((pair_cols[:, block_width:], pair_cols[:, :block_width]), axis=1)
    updated = a_trail - large_product(pair_rows, swap_cols.T)

    refl_cols = cols_from(refl)
    x_shard = product(sum_to_shard(large_product(updated, refl_cols)), g_inverse)
    core_sum, x_rows, refl_rows, x_cols = gather_both(
        rows, cols, product(refl.T, x_shard), x_shard, refl, 3
    )
    half_core = 0.5 * product(g_inverse.T, core_sum)
    z_cols = x_cols - product(refl_cols, half_core)
    z_rows = x_rows - product(refl_rows, half_core)
    trail_out = updated - large_product(
        jnp.concatenate((z_rows, refl_rows), axis=1),
        jnp.concatenate((refl_cols, z_cols), axis=1).T,
    )
    return (trail_out, panel_out)


def layer(rows, cols, *args):
    return shards(rows, cols, *args)


def solution(mesh):
    rows, cols = mesh.shape["row"], mesh.shape["col"]
    return jax.shard_map(
        functools.partial(layer, rows, cols),
        mesh=mesh,
        in_specs=(P("row", "col"), P(BOTH, None), P(BOTH, None), P(), P()),
        out_specs=(P("row", "col"), P(BOTH, None)),
        check_vma=False,
    )
```

profile of v0, /device:TPU:0, one launch (start us, length us, event | category | flops | bytes accessed | tf_op | source)
XLA Modules:
  0.0 582.8 jit_solution(8563897998537883044)
XLA Ops:
  0.7 1.5 fusion.49
  2.2 1.4 fusion.50
  3.6 1.6 fusion.10
  5.2 2.4 fusion.48
  8.5 1.1 pad_maximum_fusion
  9.6 40.5 %shard_map.68 = (f32[32,8,512]{2,1,0:T(8,128)}, f32[512,256]{1,0:T(8,128)}) custom-call(f32[32,8,512]{2,1,0:T(8,128)} %fusion.14.x_ref, f32[4096,2048]{1,0:T(8,128)} %a_ref.1), custom_call_target="tpu_custom_call" | custom-call | tf_op jit(solution)/shard_map/pallas_call | solution.py:214
  51.2 2.1 fusion.9
  56.1 28.3 %shard_map.69 = f32[32,8,512]{2,1,0:T(8,128)} custom-call(f32[32,8,512]{2,1,0:T(8,128)} %bitcast.172), custom_call_target="tpu_custom_call" | custom-call | tf_op jit(solution)/shard_map/pallas_call | solution.py:197
  85.3 1.2 copy.18
  86.8 11.7 %cholesky.50 = f32[128,128]{1,0:T(8,128)S(1)} custom-call(f32[128,128]{1,0:T(8,128)S(1)} %cholesky.118), custom_call_target="Cholesky" | custom-call | tf_op jit(solution)/shard_map/jit(cholesky)/cholesky | solution.py:452
  98.5 9.8 %custom-call.14 = f32[1,128,128]{1,2,0:T(8,128)S(1)} custom-call(f32[1,128,128]{2,1,0:T(8,128)S(1)} %get-tuple-element.50), custom_call_target="InvertDiagBlocksLowerTriangular" | custom-call | tf_op jit(solution)/shard_map/jit(cholesky)/cholesky | solution.py:452
  108.9 11.7 %cholesky.105 = f32[128,128]{1,0:T(8,128)S(1)} custom-call(f32[128,128]{1,0:T(8,128)S(1)} %convolution_subtract_fusion.13), custom_call_target="Cholesky" | custom-call | tf_op jit(solution)/shard_map/jit(cholesky)/cholesky | solution.py:452
  122.7 3.8 while.1
  123.2 1.3 bitcast_dynamic-update-slice_fusion.18
  125.2 1.3 bitcast_dynamic-update-slice_fusion.18
  126.5 19.9 %custom-call.15 = f32[2,128,128]{1,2,0:T(8,128)S(1)} custom-call(f32[2,128,128]{2,1,0:T(8,128)S(1)} %get-tuple-element.25), custom_call_target="InvertDiagBlocksLowerTriangular" | custom-call | tf_op jit(solution)/shard_map/triangular_solve | solution.py:33
  148.5 5.9 %collective-permute-start.14 = (f32[512,256]{1,0:T(8,128)S(1)}, f32[512,256]{1,0:T(8,128)}, u32[]{:S(2)}, u32[]{:S(2)}) collective-permute-start(f32[512,256]{1,0:T(8,128)S(1)} %fusion.12.v_ref), channel_id=1, source_target_pairs={{3,0},{7,1},{11,2},{15,3},{19,4},{23,5},{27,6},{31,7},{0,8},{4,9},... | collective-permute-start | bytes 1572872 | tf_op jit(solution)/shard_map/ppermute | solution.py:402
  154.4 7.6 %collective-permute-start.12 = (f32[512,256]{1,0:T(8,128)S(1)}, f32[512,256]{1,0:T(8,128)S(1)}, u32[]{:S(2)}, u32[]{:S(2)}) collective-permute-start(f32[512,256]{1,0:T(8,128)S(1)} %fusion.12.v_ref), channel_id=1, source_target_pairs={{1,0},{5,1},{9,2},{13,3},{17,4},{21,5},{25,6},{29,7},{2,8},{6,9},{... | collective-permute-start | bytes 1572872 | tf_op jit(solution)/shard_map/ppermute | solution.py:402
  162.7 3.2 collective-permute-start.9
  165.9 3.7 collective-permute-start.8
  171.8 4.3 broadcast_in_dim.77
  176.2 2.3 bitcast_dynamic-update-slice_fusion.12
  179.6 7.3 %collective-permute-start.13 = (f32[512,256]{1,0:T(8,128)S(1)}, f32[512,256]{1,0:T(8,128)}, u32[]{:S(2)}, u32[]{:S(2)}) collective-permute-start(f32[512,256]{1,0:T(8,128)S(1)} %fusion.12.v_ref), channel_id=1, source_target_pairs={{2,0},{6,1},{10,2},{14,3},{18,4},{22,5},{26,6},{30,7},{3,8},{7,9},... | collective-permute-start | bytes 1572872 | tf_op jit(solution)/shard_map/ppermute | solution.py:402
  187.0 9.4 %collective-permute-start.7 = (f32[512,512]{1,0:T(8,128)}, f32[512,512]{1,0:T(8,128)}, u32[]{:S(2)}, u32[]{:S(2)}) collective-permute-start(f32[512,512]{1,0:T(8,128)} %pad_maximum_fusion), channel_id=1, source_target_pairs={{0,0},{4,1},{8,2},{12,3},{16,4},{20,5},{24,6},{28,7},{1,8},{5,9},{... | collective-permute-start | bytes 3145736 | tf_op jit(solution)/shard_map/ppermute | solution.py:402
  199.4 25.8 %collective-permute-start.5 = (f32[512,512]{1,0:T(8,128)}, f32[512,512]{1,0:T(8,128)S(1)}, u32[]{:S(2)}, u32[]{:S(2)}) collective-permute-start(f32[512,512]{1,0:T(8,128)} %pad_maximum_fusion), channel_id=1, source_target_pairs={{0,6},{1,7},{2,0},{3,1},{4,2},{5,3},{6,4},{7,5},{8,14},{9,15},{10,... | collective-permute-start | bytes 3145736 | tf_op jit(solution)/shard_map/ppermute | solution.py:388
  225.1 46.8 %collective-permute-start.3 = (f32[512,512]{1,0:T(8,128)}, f32[512,512]{1,0:T(8,128)S(1)}, u32[]{:S(2)}, u32[]{:S(2)}) collective-permute-start(f32[512,512]{1,0:T(8,128)} %pad_maximum_fusion), channel_id=1, source_target_pairs={{0,4},{1,5},{2,6},{3,7},{4,0},{5,1},{6,2},{7,3},{8,12},{9,13},{10,... | collective-permute-start | bytes 3145736 | tf_op jit(solution)/shard_map/ppermute | solution.py:388
  273.0 4.7 collective-permute-start.10
  279.4 1.3 bitcast_dynamic-update-slice_fusion.4
  280.7 1.3 bitcast_dynamic-update-slice_fusion.3
  282.6 46.7 %collective-permute-done.3 = f32[512,512]{1,0:T(8,128)S(1)} collective-permute-done((f32[512,512]{1,0:T(8,128)}, f32[512,512]{1,0:T(8,128)S(1)}, u32[]{:S(2)}, u32[]{:S(2)}) %collective-permute-start.3) | collective-permute-done | bytes 1048608 | tf_op jit(solution)/shard_map/ppermute | solution.py:388
  329.8 1.3 bitcast_dynamic-update-slice_fusion.2
  333.3 2.3 fusion.46
  335.6 1.1 bitcast_dynamic-update-slice_fusion.9
  341.0 36.9 %convolution_subtract_fusion.1 = f32[4096,2048]{1,0:T(8,128)} fusion(f32[4096,2048]{1,0:T(8,128)} %a_ref.1, f32[4096,512]{1,0:T(8,128)} %bitcast.13, f32[2048,256]{1,0:T(8,128)} %get-tuple-element.44, f32[2048,256]{1,0:T(8,128)} %get-tuple-element.43), kind=kOutput, calls=%fused_computation.3 | convolution fusion | flops 25779240960 | bytes 79691776 | tf_op jit(solution)/shard_map/dot_general | solution.py:21
  377.9 19.3 %fusion.52 = f32[4,2,512,256]{3,2,1,0:T(8,128)} fusion(f32[4,2,512,2048]{3,2,1,0:T(8,128)} %bitcast.163, f32[2048,256,1,1]{1,0,3,2:T(8,128)S(1)} %bitcast.164), kind=kOutput, calls=%fused_computation.123 | convolution fusion | flops 12884901888 | bytes 39845888 | tf_op jit(solution)/shard_map/dot_general | solution.py:21
  397.2 2.9 dynamic-slice_bitcast_fusion.3
  403.9 2.0 bitcast_add_fusion.2
  406.0 2.9 collective-permute-start.21
  408.9 1.7 collective-permute-start.19
  411.8 9.9 %collective-permute-done.17 = f32[512,256]{1,0:T(8,128)S(1)} collective-permute-done((f32[512,256]{1,0:T(8,128)S(1)}, f32[512,256]{1,0:T(8,128)S(1)}, u32[]{:S(2)}, u32[]{:S(2)}) %collective-permute-start.17) | collective-permute-done | bytes 524320 | tf_op jit(solution)/shard_map/ppermute | solution.py:419
  421.7 10.6 %collective-permute-done.21 = f32[512,256]{1,0:T(8,128)S(1)} collective-permute-done((f32[512,256]{1,0:T(8,128)S(1)}, f32[512,256]{1,0:T(8,128)S(1)}, u32[]{:S(2)}, u32[]{:S(2)}) %collective-permute-start.21) | collective-permute-done | bytes 524320 | tf_op jit(solution)/shard_map/ppermute | solution.py:419
  432.4 1.7 fusion.21.x_ref
  434.1 1.7 convolution_bitcast_fusion.p_ref
  435.8 97.6 %shard_map.70 = (f32[32,8,256]{2,1,0:T(8,128)}, f32[8,512,256]{2,1,0:T(8,128)}, f32[8,512,256]{2,1,0:T(8,128)}, f32[4,512,256]{2,1,0:T(8,128)}) custom-call(f32[32,8,256]{2,1,0:T(8,128)} %convolution_bitcast_fusion.p_ref, f32[512,256]{1,0:T(8,128)} %copy-done.4, f32[512,256]{1,0:T(8,128)} %copy-done.3), custom_call_target="tpu_custom_call" | custom-call | tf_op jit(solution)/shard_map/pallas_call | solution.py:347
  533.4 1.3 convolution_multiply_fusion.1
  534.7 9.0 %bitcast_subtract_fusion = f32[4096,256]{1,0:T(8,128)} fusion(f32[8,512,256]{2,1,0:T(8,128)} %get-tuple-element.14, f32[4096,256]{1,0:T(8,128)} %bitcast.167, f32[256,256]{1,0:T(8,128)S(1)} %convolution_multiply_fusion.1), kind=kOutput, calls=%fused_computation.13 | convolution fusion | flops 3222274048 | bytes 12845056 | tf_op jit(solution)/shard_map/dot_general | solution.py:17
  543.8 3.2 bitcast_subtract_fusion.1
  546.9 35.6 %convolution_subtract_fusion = f32[4096,2048]{1,0:T(8,128)} fusion(f32[4096,2048]{1,0:T(8,128)} %convolution_subtract_fusion.1, f32[4096,256]{1,0:T(8,128)} %bitcast.168, f32[4096,256]{1,0:T(8,128)} %bitcast_subtract_fusion, f32[2048,256]{1,0:T(8,128)} %bitcast_subtract_fusion.1, f32[2048,256]{1,0:T(8,128)S(1)} %bitcast.166), kind=kOutput, calls=%fused_computation.2 | convolution fusion | flops 25781338112 | bytes 79691776 | tf_op jit(solution)/shard_map/dot_general | solution.py:21
  (108 shorter events, 32.4 us)
Async XLA Ops:
  0.6 4.6 copy-start
  0.6 7.0 %copy-start.2 = (f32[512,256]{1,0:T(8,128)S(1)}, f32[512,256]{1,0:T(8,128)}, u32[]{:S(2)}) copy-start(f32[512,256]{1,0:T(8,128)} %param.7) | copy-start | bytes 1572868
  148.5 285.6 %copy-start.3 = (f32[512,256]{1,0:T(8,128)}, f32[512,256]{1,0:T(8,128)S(1)}, u32[]{:S(2)}) copy-start(f32[512,256]{1,0:T(8,128)S(1)} %fusion.12.v_ref) | copy-start | bytes 1572868
  148.5 50.9 %collective-permute-start.14 = (f32[512,256]{1,0:T(8,128)S(1)}, f32[512,256]{1,0:T(8,128)}, u32[]{:S(2)}, u32[]{:S(2)}) collective-permute-start(f32[512,256]{1,0:T(8,128)S(1)} %fusion.12.v_ref), channel_id=1, source_target_pairs={{3,0},{7,1},{11,2},{15,3},{19,4},{23,5},{27,6},{31,7},{0,8},{4,9},... | collective-permute-start | bytes 1572872 | tf_op jit(solution)/shard_map/ppermute | solution.py:402
  154.4 25.2 %collective-permute-start.12 = (f32[512,256]{1,0:T(8,128)S(1)}, f32[512,256]{1,0:T(8,128)S(1)}, u32[]{:S(2)}, u32[]{:S(2)}) collective-permute-start(f32[512,256]{1,0:T(8,128)S(1)} %fusion.12.v_ref), channel_id=1, source_target_pairs={{1,0},{5,1},{9,2},{13,3},{17,4},{21,5},{25,6},{29,7},{2,8},{6,9},{... | collective-permute-start | bytes 1572872 | tf_op jit(solution)/shard_map/ppermute | solution.py:402
  162.0 25.0 %collective-permute-start.11 = (f32[512,256]{1,0:T(8,128)S(1)}, f32[512,256]{1,0:T(8,128)S(1)}, u32[]{:S(2)}, u32[]{:S(2)}) collective-permute-start(f32[512,256]{1,0:T(8,128)S(1)} %fusion.12.v_ref), channel_id=1, source_target_pairs={{0,0},{4,1},{8,2},{12,3},{16,4},{20,5},{24,6},{28,7},{1,8},{5,9},{... | collective-permute-start | bytes 1572872 | tf_op jit(solution)/shard_map/ppermute | solution.py:402
  162.7 109.2 %collective-permute-start.9 = (f32[512,512]{1,0:T(8,128)}, f32[512,512]{1,0:T(8,128)}, u32[]{:S(2)}, u32[]{:S(2)}) collective-permute-start(f32[512,512]{1,0:T(8,128)} %pad_maximum_fusion), channel_id=1, source_target_pairs={{2,0},{6,1},{10,2},{14,3},{18,4},{22,5},{26,6},{30,7},{3,8},{7,9},... | collective-permute-start | bytes 3145736 | tf_op jit(solution)/shard_map/ppermute | solution.py:402
  165.9 107.1 %collective-permute-start.8 = (f32[512,512]{1,0:T(8,128)}, f32[512,512]{1,0:T(8,128)}, u32[]{:S(2)}, u32[]{:S(2)}) collective-permute-start(f32[512,512]{1,0:T(8,128)} %pad_maximum_fusion), channel_id=1, source_target_pairs={{1,0},{5,1},{9,2},{13,3},{17,4},{21,5},{25,6},{29,7},{2,8},{6,9},{... | collective-permute-start | bytes 3145736 | tf_op jit(solution)/shard_map/ppermute | solution.py:402
  179.6 17.4 %copy-start.6 = (f32[512,256]{1,0:T(8,128)}, f32[512,256]{1,0:T(8,128)S(1)}, u32[]{:S(2)}) copy-start(f32[512,256]{1,0:T(8,128)S(1)} %collective-permute-done.12) | copy-start | bytes 1572868
  179.6 45.5 %collective-permute-start.13 = (f32[512,256]{1,0:T(8,128)S(1)}, f32[512,256]{1,0:T(8,128)}, u32[]{:S(2)}, u32[]{:S(2)}) collective-permute-start(f32[512,256]{1,0:T(8,128)S(1)} %fusion.12.v_ref), channel_id=1, source_target_pairs={{2,0},{6,1},{10,2},{14,3},{18,4},{22,5},{26,6},{30,7},{3,8},{7,9},... | collective-permute-start | bytes 1572872 | tf_op jit(solution)/shard_map/ppermute | solution.py:402
  187.0 10.1 %copy-start.7 = (f32[512,256]{1,0:T(8,128)}, f32[512,256]{1,0:T(8,128)S(1)}, u32[]{:S(2)}) copy-start(f32[512,256]{1,0:T(8,128)S(1)} %collective-permute-done.11) | copy-start | bytes 1572868
  187.0 91.8 %collective-permute-start.7 = (f32[512,512]{1,0:T(8,128)}, f32[512,512]{1,0:T(8,128)}, u32[]{:S(2)}, u32[]{:S(2)}) collective-permute-start(f32[512,512]{1,0:T(8,128)} %pad_maximum_fusion), channel_id=1, source_target_pairs={{0,0},{4,1},{8,2},{12,3},{16,4},{20,5},{24,6},{28,7},{1,8},{5,9},{... | collective-permute-start | bytes 3145736 | tf_op jit(solution)/shard_map/ppermute | solution.py:402
  199.4 82.7 %collective-permute-start.5 = (f32[512,512]{1,0:T(8,128)}, f32[512,512]{1,0:T(8,128)S(1)}, u32[]{:S(2)}, u32[]{:S(2)}) collective-permute-start(f32[512,512]{1,0:T(8,128)} %pad_maximum_fusion), channel_id=1, source_target_pairs={{0,6},{1,7},{2,0},{3,1},{4,2},{5,3},{6,4},{7,5},{8,14},{9,15},{10,... | collective-permute-start | bytes 3145736 | tf_op jit(solution)/shard_map/ppermute | solution.py:388
  225.1 104.2 %collective-permute-start.3 = (f32[512,512]{1,0:T(8,128)}, f32[512,512]{1,0:T(8,128)S(1)}, u32[]{:S(2)}, u32[]{:S(2)}) collective-permute-start(f32[512,512]{1,0:T(8,128)} %pad_maximum_fusion), channel_id=1, source_target_pairs={{0,4},{1,5},{2,6},{3,7},{4,0},{5,1},{6,2},{7,3},{8,12},{9,13},{10,... | collective-permute-start | bytes 3145736 | tf_op jit(solution)/shard_map/ppermute | solution.py:388
  271.9 57.4 %collective-permute-start.1 = (f32[512,512]{1,0:T(8,128)}, f32[512,512]{1,0:T(8,128)S(1)}, u32[]{:S(2)}, u32[]{:S(2)}) collective-permute-start(f32[512,512]{1,0:T(8,128)} %pad_maximum_fusion), channel_id=1, source_target_pairs={{0,2},{1,3},{2,4},{3,5},{4,6},{5,7},{6,0},{7,1},{8,10},{9,11},{10,... | collective-permute-start | bytes 3145736 | tf_op jit(solution)/shard_map/ppermute | solution.py:388
  273.0 58.1 %collective-permute-start.10 = (f32[512,512]{1,0:T(8,128)}, f32[512,512]{1,0:T(8,128)S(1)}, u32[]{:S(2)}, u32[]{:S(2)}) collective-permute-start(f32[512,512]{1,0:T(8,128)} %pad_maximum_fusion), channel_id=1, source_target_pairs={{3,0},{7,1},{11,2},{15,3},{19,4},{23,5},{27,6},{31,7},{0,8},{4,9},... | collective-permute-start | bytes 3145736 | tf_op jit(solution)/shard_map/ppermute | solution.py:402
  278.8 52.4 %collective-permute-start = (f32[512,512]{1,0:T(8,128)}, f32[512,512]{1,0:T(8,128)S(1)}, u32[]{:S(2)}, u32[]{:S(2)}) collective-permute-start(f32[512,512]{1,0:T(8,128)} %pad_maximum_fusion), channel_id=1, source_target_pairs={{0,1},{1,0},{2,3},{3,2},{4,5},{5,4},{6,7},{7,6},{8,9},{9,8},{10,11... | collective-permute-start | bytes 3145736 | tf_op jit(solution)/shard_map/ppermute | solution.py:389
  282.0 57.9 %collective-permute-start.6 = (f32[512,512]{1,0:T(8,128)S(1)}, f32[512,512]{1,0:T(8,128)S(1)}, u32[]{:S(2)}, u32[]{:S(2)}) collective-permute-start(f32[512,512]{1,0:T(8,128)S(1)} %collective-permute-done.5), channel_id=1, source_target_pairs={{0,1},{1,0},{2,3},{3,2},{4,5},{5,4},{6,7},{7,6},{8,9},{9,8},{10,11... | collective-permute-start | bytes 3145736 | tf_op jit(solution)/shard_map/ppermute | solution.py:389
  329.3 8.5 %collective-permute-start.4 = (f32[512,512]{1,0:T(8,128)S(1)}, f32[512,512]{1,0:T(8,128)S(1)}, u32[]{:S(2)}, u32[]{:S(2)}) collective-permute-start(f32[512,512]{1,0:T(8,128)S(1)} %collective-permute-done.3), channel_id=1, source_target_pairs={{0,1},{1,0},{2,3},{3,2},{4,5},{5,4},{6,7},{7,6},{8,9},{9,8},{10,11... | collective-permute-start | bytes 3145736 | tf_op jit(solution)/shard_map/ppermute | solution.py:389
  329.3 6.3 %collective-permute-start.2 = (f32[512,512]{1,0:T(8,128)S(1)}, f32[512,512]{1,0:T(8,128)S(1)}, u32[]{:S(2)}, u32[]{:S(2)}) collective-permute-start(f32[512,512]{1,0:T(8,128)S(1)} %collective-permute-done.1), channel_id=1, source_target_pairs={{0,1},{1,0},{2,3},{3,2},{4,5},{5,4},{6,7},{7,6},{8,9},{9,8},{10,11... | collective-permute-start | bytes 3145736 | tf_op jit(solution)/shard_map/ppermute | solution.py:389
  400.2 2.3 collective-permute-start.20
  400.2 3.0 collective-permute-start.18
  400.7 3.2 collective-permute-start.16
  401.9 9.9 %collective-permute-start.15 = (f32[512,256]{1,0:T(8,128)}, f32[512,256]{1,0:T(8,128)S(1)}, u32[]{:S(2)}, u32[]{:S(2)}) collective-permute-start(f32[512,256]{1,0:T(8,128)} %get-tuple-element.36), channel_id=1, source_target_pairs={{0,1},{1,0},{2,3},{3,2},{4,5},{5,4},{6,7},{7,6},{8,9},{9,8},{10,11... | collective-permute-start | bytes 1572872 | tf_op jit(solution)/shard_map/ppermute | solution.py:417
  405.9 15.8 %collective-permute-start.17 = (f32[512,256]{1,0:T(8,128)S(1)}, f32[512,256]{1,0:T(8,128)S(1)}, u32[]{:S(2)}, u32[]{:S(2)}) collective-permute-start(f32[512,256]{1,0:T(8,128)S(1)} %get-tuple-element.40), channel_id=1, source_target_pairs={{0,2},{1,3},{2,4},{3,5},{4,6},{5,7},{6,0},{7,1},{8,10},{9,11},{10,... | collective-permute-start | bytes 1572872 | tf_op jit(solution)/shard_map/ppermute | solution.py:419
  406.0 26.4 %collective-permute-start.21 = (f32[512,256]{1,0:T(8,128)S(1)}, f32[512,256]{1,0:T(8,128)S(1)}, u32[]{:S(2)}, u32[]{:S(2)}) collective-permute-start(f32[512,256]{1,0:T(8,128)S(1)} %get-tuple-element.41), channel_id=1, source_target_pairs={{0,6},{1,7},{2,0},{3,1},{4,2},{5,3},{6,4},{7,5},{8,14},{9,15},{10,... | collective-permute-start | bytes 1572872 | tf_op jit(solution)/shard_map/ppermute | solution.py:419
  408.9 23.5 %collective-permute-start.19 = (f32[512,256]{1,0:T(8,128)S(1)}, f32[512,256]{1,0:T(8,128)S(1)}, u32[]{:S(2)}, u32[]{:S(2)}) collective-permute-start(f32[512,256]{1,0:T(8,128)S(1)} %get-tuple-element.42), channel_id=1, source_target_pairs={{0,4},{1,5},{2,6},{3,7},{4,0},{5,1},{6,2},{7,3},{8,12},{9,13},{10,... | collective-permute-start | bytes 1572872 | tf_op jit(solution)/shard_map/ppermute | solution.py:419
  434.1 1.7 copy-start.4
  534.7 9.0 %copy-start.5 = (f32[4,512,256]{2,1,0:T(8,128)S(1)}, f32[4,512,256]{2,1,0:T(8,128)}, u32[]{:S(2)}) copy-start(f32[4,512,256]{2,1,0:T(8,128)} %get-tuple-element.17) | copy-start | bytes 6291460
  546.9 35.6 %copy-start.1 = (f32[512,256]{1,0:T(8,128)S(1)}, f32[512,256]{1,0:T(8,128)}, u32[]{:S(2)}) copy-start(f32[512,256]{1,0:T(8,128)} %param.6) | copy-start | bytes 1572868
where the time goes:
time: 589 us; the launch traced here: 583 us
  Pallas kernels  166 us (28%)
  matrix products  128 us (22%)
  starting transfers between devices  122 us (21%)
  waiting for transfers between devices  68.8 us (12%)
  other arithmetic  58.2 us (10%)
  local copies, waits for them, and re-layouts  36.8 us (6%)
    pallas_call x1, Pallas kernels, gather_both(): pl.pallas_call(functools.partial(gather_kernel, rows, cols), out_shape=(j...  97.6 us
    dot_general x3, matrix products, large_product(): jnp.dot(left, right, precision=lax.Precision.HIGH, preferred_element_type...  91.8 us
    ppermute x3, starting transfers between devices, rows_from(): part = lax.ppermute(shard, 'col', chip_shift(step)) if step else shard  72.5 us
    ppermute x3, waiting for transfers between devices, rows_from(): part = lax.ppermute(shard, 'col', chip_shift(step)) if step else shard  46.7 us
    ppermute x8, starting transfers between devices, cols_from(): part = lax.ppermute(shard, BOTH, pairs)  42.6 us
    pallas_call x1, Pallas kernels, first_exchange(): pl.pallas_call(functools.partial(first_kernel, rows, cols, held), out_sha...  40.5 us
    another operation x6, other arithmetic, shards(): factor = jnp.linalg.cholesky(stats[:, :block_width])  34 us
    dot_general x28, matrix products, product(): jnp.dot(left, right, precision=lax.Precision.HIGHEST, preferred_element_t...  33.5 us
  transfers between devices with their start and end apart: 22, of which 5 were waited for; matrix products, arithmetic and copies ran while one was open for 6% of the time, Pallas kernels for 0%

commit v1 on v0

--- a/solution.py
+++ b/solution.py
@@ -468,10 +468,9 @@
         rows, cols, product(refl.T, x_shard), x_shard, refl, 3
     )
     half_core = 0.5 * product(g_inverse.T, core_sum)
-    z_cols = x_cols - product(refl_cols, half_core)
-    z_rows = x_rows - product(refl_rows, half_core)
+    z_cols = x_cols - product(refl_cols, half_core + half_core.T)
     trail_out = updated - large_product(
-        jnp.concatenate((z_rows, refl_rows), axis=1),
+        jnp.concatenate((x_rows, refl_rows), axis=1),
         jnp.concatenate((refl_cols, z_cols), axis=1).T,
     )
     return (trail_out, panel_out)

time: 589 us -> 570 us (0.968)
  starting transfers between devices: 122 us -> 86.3 us
  waiting for transfers between devices: 68.8 us -> 97.3 us
  matrix products: 128 us -> 120 us
    ppermute x3, starting transfers between devices: 72.5 us -> 17.8 us  [rows_from(): part = lax.ppermute(shard, 'col', chip_shift(step)) if step else shard]
    ppermute x8, waiting for transfers between devices: 0.02 us -> 40.1 us  [cols_from(): part = lax.ppermute(shard, BOTH, pairs)]
    ppermute x3, starting transfers between devices: 4.66 us -> 36.8 us  [sum_to_shard(): both = lax.ppermute(both, 'col', chip_shift(step))]
    ppermute x8, starting transfers between devices: 42.6 us -> 29.3 us  [cols_from(): part = lax.ppermute(shard, BOTH, pairs)]
    ppermute x3, waiting for transfers between devices: 46.7 us -> 34.3 us  [rows_from(): part = lax.ppermute(shard, 'col', chip_shift(step)) if step else shard]
    dot_general x28 -> x27, matrix products: 33.5 us -> 26 us  [product(): jnp.dot(left, right, precision=lax.Precision.HIGHEST, preferred_element_t...]
  transfers between devices with their start and end apart: 22 -> 22, of which waited for: 5 -> 9; matrix products, arithmetic and copies ran while one was open for 6% -> 16% of each run, Pallas kernels for 0% -> 0%
where the time goes in v1:
time: 570 us; the launch traced here: 563 us
  Pallas kernels  163 us (29%)
  matrix products  120 us (21%)
  waiting for transfers between devices  97.3 us (17%)
  starting transfers between devices  86.3 us (15%)
  other arithmetic  58 us (10%)
  local copies, waits for them, and re-layouts  35.7 us (6%)
    pallas_call x1, Pallas kernels, gather_both(): pl.pallas_call(functools.partial(gather_kernel, rows, cols), out_shape=(j...  93.9 us
    dot_general x3, matrix products, large_product(): jnp.dot(left, right, precision=lax.Precision.HIGH, preferred_element_type...  91.7 us
    pallas_call x1, Pallas kernels, first_exchange(): pl.pallas_call(functools.partial(first_kernel, rows, cols, held), out_sha...  40.5 us
    ppermute x8, waiting for transfers between devices, cols_from(): part = lax.ppermute(shard, BOTH, pairs)  40.1 us
    ppermute x3, starting transfers between devices, sum_to_shard(): both = lax.ppermute(both, 'col', chip_shift(step))  36.8 us
    ppermute x3, waiting for transfers between devices, rows_from(): part = lax.ppermute(shard, 'col', chip_shift(step)) if step else shard  34.3 us
    another operation x6, other arithmetic, shards(): factor = jnp.linalg.cholesky(stats[:, :block_width])  34 us
    ppermute x8, starting transfers between devices, cols_from(): part = lax.ppermute(shard, BOTH, pairs)  29.3 us
  transfers between devices with their start and end apart: 22, of which 9 were waited for; matrix products, arithmetic and copies ran while one was open for 16% of the time, Pallas kernels for 0%

profile of v1, /device:TPU:0, one launch (start us, length us, event | category | flops | bytes accessed | tf_op | source)
XLA Modules:
  0.0 563.2 jit_solution(5617570819018899432)
XLA Ops:
  0.7 1.5 fusion.57
  2.2 1.4 fusion.58
  3.5 1.6 fusion.10
  5.2 2.4 fusion.56
  9.6 40.5 %shard_map.68 = (f32[32,8,512]{2,1,0:T(8,128)}, f32[512,256]{1,0:T(8,128)}) custom-call(f32[32,8,512]{2,1,0:T(8,128)} %fusion.14.x_ref, f32[4096,2048]{1,0:T(8,128)} %a_ref.1), custom_call_target="tpu_custom_call" | custom-call | tf_op jit(solution)/shard_map/pallas_call | solution.py:214
  51.2 2.1 fusion.9
  56.1 28.3 %shard_map.69 = f32[32,8,512]{2,1,0:T(8,128)} custom-call(f32[32,8,512]{2,1,0:T(8,128)} %bitcast.175), custom_call_target="tpu_custom_call" | custom-call | tf_op jit(solution)/shard_map/pallas_call | solution.py:197
  84.8 9.6 %collective-permute-start.7 = (f32[512,512]{1,0:T(8,128)}, f32[512,512]{1,0:T(8,128)}, u32[]{:S(2)}, u32[]{:S(2)}) collective-permute-start(f32[512,512]{1,0:T(8,128)} %pad_maximum_fusion), channel_id=1, source_target_pairs={{0,0},{4,1},{8,2},{12,3},{16,4},{20,5},{24,6},{28,7},{1,8},{5,9},{... | collective-permute-start | bytes 3145736 | tf_op jit(solution)/shard_map/ppermute | solution.py:402
  95.5 1.2 copy.19
  96.9 11.7 %cholesky.50 = f32[128,128]{1,0:T(8,128)S(1)} custom-call(f32[128,128]{1,0:T(8,128)S(1)} %cholesky.118), custom_call_target="Cholesky" | custom-call | tf_op jit(solution)/shard_map/jit(cholesky)/cholesky | solution.py:452
  108.7 9.8 %custom-call.14 = f32[1,128,128]{1,2,0:T(8,128)S(1)} custom-call(f32[1,128,128]{2,1,0:T(8,128)S(1)} %get-tuple-element.50), custom_call_target="InvertDiagBlocksLowerTriangular" | custom-call | tf_op jit(solution)/shard_map/jit(cholesky)/cholesky | solution.py:452
  119.0 11.7 %cholesky.105 = f32[128,128]{1,0:T(8,128)S(1)} custom-call(f32[128,128]{1,0:T(8,128)S(1)} %convolution_subtract_fusion.13), custom_call_target="Cholesky" | custom-call | tf_op jit(solution)/shard_map/jit(cholesky)/cholesky | solution.py:452
  132.9 4.3 while.1
  133.7 1.3 bitcast_dynamic-update-slice_fusion.18
  135.8 1.3 bitcast_dynamic-update-slice_fusion.18
  137.2 19.7 %custom-call.15 = f32[2,128,128]{1,2,0:T(8,128)S(1)} custom-call(f32[2,128,128]{2,1,0:T(8,128)S(1)} %get-tuple-element.25), custom_call_target="InvertDiagBlocksLowerTriangular" | custom-call | tf_op jit(solution)/shard_map/triangular_solve | solution.py:33
  159.7 5.1 collective-permute-start.12
  164.7 4.1 collective-permute-start.13
  171.4 4.3 broadcast_in_dim.77
  175.8 2.3 bitcast_dynamic-update-slice_fusion.12
  179.5 8.8 %collective-permute-start.1 = (f32[512,512]{1,0:T(8,128)}, f32[512,512]{1,0:T(8,128)S(1)}, u32[]{:S(2)}, u32[]{:S(2)}) collective-permute-start(f32[512,512]{1,0:T(8,128)} %pad_maximum_fusion), channel_id=1, source_target_pairs={{0,2},{1,3},{2,4},{3,5},{4,6},{5,7},{6,0},{7,1},{8,10},{9,11},{10,... | collective-permute-start | bytes 3145736 | tf_op jit(solution)/shard_map/ppermute | solution.py:388
  189.1 5.3 collective-permute-start.14
  196.7 9.1 %collective-permute-start.3 = (f32[512,512]{1,0:T(8,128)}, f32[512,512]{1,0:T(8,128)S(1)}, u32[]{:S(2)}, u32[]{:S(2)}) collective-permute-start(f32[512,512]{1,0:T(8,128)} %pad_maximum_fusion), channel_id=1, source_target_pairs={{0,4},{1,5},{2,6},{3,7},{4,0},{5,1},{6,2},{7,3},{8,12},{9,13},{10,... | collective-permute-start | bytes 3145736 | tf_op jit(solution)/shard_map/ppermute | solution.py:388
  206.9 25.5 %collective-permute-done.14 = f32[512,256]{1,0:T(8,128)S(1)} collective-permute-done((f32[512,256]{1,0:T(8,128)S(1)}, f32[512,256]{1,0:T(8,128)S(1)}, u32[]{:S(2)}, u32[]{:S(2)}) %collective-permute-start.14) | collective-permute-done | bytes 524320 | tf_op jit(solution)/shard_map/ppermute | solution.py:402
  232.4 1.9 collective-permute-start.8
  234.9 1.3 bitcast_dynamic-update-slice_fusion.4
  236.2 2.5 collective-permute-start.10
  238.7 2.3 bitcast_dynamic-update-slice_fusion.11
  242.0 17.4 %collective-permute-done.3 = f32[512,512]{1,0:T(8,128)S(1)} collective-permute-done((f32[512,512]{1,0:T(8,128)}, f32[512,512]{1,0:T(8,128)S(1)}, u32[]{:S(2)}, u32[]{:S(2)}) %collective-permute-start.3) | collective-permute-done | bytes 1048608 | tf_op jit(solution)/shard_map/ppermute | solution.py:388
  259.6 16.9 %collective-permute-done.5 = f32[512,512]{1,0:T(8,128)S(1)} collective-permute-done((f32[512,512]{1,0:T(8,128)}, f32[512,512]{1,0:T(8,128)S(1)}, u32[]{:S(2)}, u32[]{:S(2)}) %collective-permute-start.5) | collective-permute-done | bytes 1048608 | tf_op jit(solution)/shard_map/ppermute | solution.py:388
  277.1 3.5 collective-permute-done.9
  280.7 11.2 %collective-permute-done.10 = f32[512,512]{1,0:T(8,128)S(1)} collective-permute-done((f32[512,512]{1,0:T(8,128)}, f32[512,512]{1,0:T(8,128)S(1)}, u32[]{:S(2)}, u32[]{:S(2)}) %collective-permute-start.10) | collective-permute-done | bytes 1048608 | tf_op jit(solution)/shard_map/ppermute | solution.py:402
  291.9 2.3 fusion.54
  299.6 37.0 %convolution_subtract_fusion.1 = f32[4096,2048]{1,0:T(8,128)} fusion(f32[4096,2048]{1,0:T(8,128)} %a_ref.1, f32[4096,512]{1,0:T(8,128)} %bitcast.13, f32[2048,256]{1,0:T(8,128)} %get-tuple-element.44, f32[2048,256]{1,0:T(8,128)} %get-tuple-element.43), kind=kOutput, calls=%fused_computation.3 | convolution fusion | flops 25779240960 | bytes 79691776 | tf_op jit(solution)/shard_map/dot_general | solution.py:21
  336.6 19.3 %fusion.60 = f32[4,2,512,256]{3,2,1,0:T(8,128)} fusion(f32[4,2,512,2048]{3,2,1,0:T(8,128)} %bitcast.166, f32[2048,256,1,1]{1,0,3,2:T(8,128)S(1)} %bitcast.167), kind=kOutput, calls=%fused_computation.127 | convolution fusion | flops 12884901888 | bytes 39845888 | tf_op jit(solution)/shard_map/dot_general | solution.py:21
  355.9 2.9 dynamic-slice_bitcast_fusion.3
  362.5 2.0 bitcast_add_fusion.2
  364.6 2.6 collective-permute-start.21
  367.2 32.2 %collective-permute-start.19 = (f32[512,256]{1,0:T(8,128)S(1)}, f32[512,256]{1,0:T(8,128)S(1)}, u32[]{:S(2)}, u32[]{:S(2)}) collective-permute-start(f32[512,256]{1,0:T(8,128)S(1)} %get-tuple-element.42), channel_id=1, source_target_pairs={{0,4},{1,5},{2,6},{3,7},{4,0},{5,1},{6,2},{7,3},{8,12},{9,13},{10,... | collective-permute-start | bytes 1572872 | tf_op jit(solution)/shard_map/ppermute | solution.py:419
  399.4 1.9 collective-permute-start.17
  402.6 19.6 %collective-permute-done.19 = f32[512,256]{1,0:T(8,128)S(1)} collective-permute-done((f32[512,256]{1,0:T(8,128)S(1)}, f32[512,256]{1,0:T(8,128)S(1)}, u32[]{:S(2)}, u32[]{:S(2)}) %collective-permute-start.19) | collective-permute-done | bytes 524320 | tf_op jit(solution)/shard_map/ppermute | solution.py:419
  422.2 1.8 collective-permute-done.17
  424.0 1.7 fusion.21.x_ref
  425.7 1.7 convolution_bitcast_fusion.p_ref
  427.4 93.9 %shard_map.70 = (f32[32,8,256]{2,1,0:T(8,128)}, f32[8,512,256]{2,1,0:T(8,128)}, f32[8,512,256]{2,1,0:T(8,128)}, f32[4,512,256]{2,1,0:T(8,128)}) custom-call(f32[32,8,256]{2,1,0:T(8,128)} %convolution_bitcast_fusion.p_ref, f32[512,256]{1,0:T(8,128)} %copy-done.4, f32[512,256]{1,0:T(8,128)} %copy-done.3), custom_call_target="tpu_custom_call" | custom-call | tf_op jit(solution)/shard_map/pallas_call | solution.py:347
  521.3 1.3 fusion.34
  522.8 4.8 bitcast_subtract_fusion
  527.5 35.5 %convolution_subtract_fusion = f32[4096,2048]{1,0:T(8,128)} fusion(f32[4096,2048]{1,0:T(8,128)} %convolution_subtract_fusion.1, f32[4096,256]{1,0:T(8,128)} %bitcast.172, f32[4096,256]{1,0:T(8,128)} %bitcast.171, f32[2048,256]{1,0:T(8,128)} %bitcast_subtract_fusion, f32[2048,256]{1,0:T(8,128)S(1)} %bitcast.169), kind=kOutput, calls=%fused_computation.2 | convolution fusion | flops 25781338112 | bytes 79691776 | tf_op jit(solution)/shard_map/dot_general | solution.py:21
  (106 shorter events, 33.8 us)
Async XLA Ops:
  0.6 4.6 copy-start
  0.6 6.9 %copy-start.2 = (f32[512,256]{1,0:T(8,128)S(1)}, f32[512,256]{1,0:T(8,128)}, u32[]{:S(2)}) copy-start(f32[512,256]{1,0:T(8,128)} %param.7) | copy-start | bytes 1572868
  84.3 148.0 %collective-permute-start = (f32[512,512]{1,0:T(8,128)}, f32[512,512]{1,0:T(8,128)}, u32[]{:S(2)}, u32[]{:S(2)}) collective-permute-start(f32[512,512]{1,0:T(8,128)} %pad_maximum_fusion), channel_id=1, source_target_pairs={{0,1},{1,0},{2,3},{3,2},{4,5},{5,4},{6,7},{7,6},{8,9},{9,8},{10,11... | collective-permute-start | bytes 3145736 | tf_op jit(solution)/shard_map/ppermute | solution.py:389
  84.8 149.5 %collective-permute-start.7 = (f32[512,512]{1,0:T(8,128)}, f32[512,512]{1,0:T(8,128)}, u32[]{:S(2)}, u32[]{:S(2)}) collective-permute-start(f32[512,512]{1,0:T(8,128)} %pad_maximum_fusion), channel_id=1, source_target_pairs={{0,0},{4,1},{8,2},{12,3},{16,4},{20,5},{24,6},{28,7},{1,8},{5,9},{... | collective-permute-start | bytes 3145736 | tf_op jit(solution)/shard_map/ppermute | solution.py:402
  158.9 266.8 %copy-start.3 = (f32[512,256]{1,0:T(8,128)}, f32[512,256]{1,0:T(8,128)S(1)}, u32[]{:S(2)}) copy-start(f32[512,256]{1,0:T(8,128)S(1)} %fusion.12.v_ref) | copy-start | bytes 1572868
  159.0 20.5 %collective-permute-start.11 = (f32[512,256]{1,0:T(8,128)S(1)}, f32[512,256]{1,0:T(8,128)S(1)}, u32[]{:S(2)}, u32[]{:S(2)}) collective-permute-start(f32[512,256]{1,0:T(8,128)S(1)} %fusion.12.v_ref), channel_id=1, source_target_pairs={{0,0},{4,1},{8,2},{12,3},{16,4},{20,5},{24,6},{28,7},{1,8},{5,9},{... | collective-permute-start | bytes 1572872 | tf_op jit(solution)/shard_map/ppermute | solution.py:402
  159.7 28.6 %collective-permute-start.12 = (f32[512,256]{1,0:T(8,128)S(1)}, f32[512,256]{1,0:T(8,128)S(1)}, u32[]{:S(2)}, u32[]{:S(2)}) collective-permute-start(f32[512,256]{1,0:T(8,128)S(1)} %fusion.12.v_ref), channel_id=1, source_target_pairs={{1,0},{5,1},{9,2},{13,3},{17,4},{21,5},{25,6},{29,7},{2,8},{6,9},{... | collective-permute-start | bytes 1572872 | tf_op jit(solution)/shard_map/ppermute | solution.py:402
  164.7 32.0 %collective-permute-start.13 = (f32[512,256]{1,0:T(8,128)S(1)}, f32[512,256]{1,0:T(8,128)}, u32[]{:S(2)}, u32[]{:S(2)}) collective-permute-start(f32[512,256]{1,0:T(8,128)S(1)} %fusion.12.v_ref), channel_id=1, source_target_pairs={{2,0},{6,1},{10,2},{14,3},{18,4},{22,5},{26,6},{30,7},{3,8},{7,9},... | collective-permute-start | bytes 1572872 | tf_op jit(solution)/shard_map/ppermute | solution.py:402
  179.5 8.8 %copy-start.5 = (f32[512,256]{1,0:T(8,128)}, f32[512,256]{1,0:T(8,128)S(1)}, u32[]{:S(2)}) copy-start(f32[512,256]{1,0:T(8,128)S(1)} %collective-permute-done.11) | copy-start | bytes 1572868
  179.5 56.8 %collective-permute-start.1 = (f32[512,512]{1,0:T(8,128)}, f32[512,512]{1,0:T(8,128)S(1)}, u32[]{:S(2)}, u32[]{:S(2)}) collective-permute-start(f32[512,512]{1,0:T(8,128)} %pad_maximum_fusion), channel_id=1, source_target_pairs={{0,2},{1,3},{2,4},{3,5},{4,6},{5,7},{6,0},{7,1},{8,10},{9,11},{10,... | collective-permute-start | bytes 3145736 | tf_op jit(solution)/shard_map/ppermute | solution.py:388
  188.3 0.8 copy-start.6
  189.1 43.2 %collective-permute-start.14 = (f32[512,256]{1,0:T(8,128)S(1)}, f32[512,256]{1,0:T(8,128)S(1)}, u32[]{:S(2)}, u32[]{:S(2)}) collective-permute-start(f32[512,256]{1,0:T(8,128)S(1)} %fusion.12.v_ref), channel_id=1, source_target_pairs={{3,0},{7,1},{11,2},{15,3},{19,4},{23,5},{27,6},{31,7},{0,8},{4,9},... | collective-permute-start | bytes 1572872 | tf_op jit(solution)/shard_map/ppermute | solution.py:402
  196.7 62.6 %collective-permute-start.3 = (f32[512,512]{1,0:T(8,128)}, f32[512,512]{1,0:T(8,128)S(1)}, u32[]{:S(2)}, u32[]{:S(2)}) collective-permute-start(f32[512,512]{1,0:T(8,128)} %pad_maximum_fusion), channel_id=1, source_target_pairs={{0,4},{1,5},{2,6},{3,7},{4,0},{5,1},{6,2},{7,3},{8,12},{9,13},{10,... | collective-permute-start | bytes 3145736 | tf_op jit(solution)/shard_map/ppermute | solution.py:388
  232.3 44.2 %collective-permute-start.5 = (f32[512,512]{1,0:T(8,128)}, f32[512,512]{1,0:T(8,128)S(1)}, u32[]{:S(2)}, u32[]{:S(2)}) collective-permute-start(f32[512,512]{1,0:T(8,128)} %pad_maximum_fusion), channel_id=1, source_target_pairs={{0,6},{1,7},{2,0},{3,1},{4,2},{5,3},{6,4},{7,5},{8,14},{9,15},{10,... | collective-permute-start | bytes 3145736 | tf_op jit(solution)/shard_map/ppermute | solution.py:388
  232.4 44.2 %collective-permute-start.8 = (f32[512,512]{1,0:T(8,128)}, f32[512,512]{1,0:T(8,128)S(1)}, u32[]{:S(2)}, u32[]{:S(2)}) collective-permute-start(f32[512,512]{1,0:T(8,128)} %pad_maximum_fusion), channel_id=1, source_target_pairs={{1,0},{5,1},{9,2},{13,3},{17,4},{21,5},{25,6},{29,7},{2,8},{6,9},{... | collective-permute-start | bytes 3145736 | tf_op jit(solution)/shard_map/ppermute | solution.py:402
  234.3 46.3 %collective-permute-start.9 = (f32[512,512]{1,0:T(8,128)}, f32[512,512]{1,0:T(8,128)S(1)}, u32[]{:S(2)}, u32[]{:S(2)}) collective-permute-start(f32[512,512]{1,0:T(8,128)} %pad_maximum_fusion), channel_id=1, source_target_pairs={{2,0},{6,1},{10,2},{14,3},{18,4},{22,5},{26,6},{30,7},{3,8},{7,9},... | collective-permute-start | bytes 3145736 | tf_op jit(solution)/shard_map/ppermute | solution.py:402
  236.2 55.6 %collective-permute-start.10 = (f32[512,512]{1,0:T(8,128)}, f32[512,512]{1,0:T(8,128)S(1)}, u32[]{:S(2)}, u32[]{:S(2)}) collective-permute-start(f32[512,512]{1,0:T(8,128)} %pad_maximum_fusion), channel_id=1, source_target_pairs={{3,0},{7,1},{11,2},{15,3},{19,4},{23,5},{27,6},{31,7},{0,8},{4,9},... | collective-permute-start | bytes 3145736 | tf_op jit(solution)/shard_map/ppermute | solution.py:402
  259.4 34.9 %collective-permute-start.2 = (f32[512,512]{1,0:T(8,128)S(1)}, f32[512,512]{1,0:T(8,128)S(1)}, u32[]{:S(2)}, u32[]{:S(2)}) collective-permute-start(f32[512,512]{1,0:T(8,128)S(1)} %collective-permute-done.1), channel_id=1, source_target_pairs={{0,1},{1,0},{2,3},{3,2},{4,5},{5,4},{6,7},{7,6},{8,9},{9,8},{10,11... | collective-permute-start | bytes 3145736 | tf_op jit(solution)/shard_map/ppermute | solution.py:389
  276.5 19.9 %collective-permute-start.4 = (f32[512,512]{1,0:T(8,128)S(1)}, f32[512,512]{1,0:T(8,128)S(1)}, u32[]{:S(2)}, u32[]{:S(2)}) collective-permute-start(f32[512,512]{1,0:T(8,128)S(1)} %collective-permute-done.3), channel_id=1, source_target_pairs={{0,1},{1,0},{2,3},{3,2},{4,5},{5,4},{6,7},{7,6},{8,9},{9,8},{10,11... | collective-permute-start | bytes 3145736 | tf_op jit(solution)/shard_map/ppermute | solution.py:389
  276.5 22.0 %collective-permute-start.6 = (f32[512,512]{1,0:T(8,128)S(1)}, f32[512,512]{1,0:T(8,128)S(1)}, u32[]{:S(2)}, u32[]{:S(2)}) collective-permute-start(f32[512,512]{1,0:T(8,128)S(1)} %collective-permute-done.5), channel_id=1, source_target_pairs={{0,1},{1,0},{2,3},{3,2},{4,5},{5,4},{6,7},{7,6},{8,9},{9,8},{10,11... | collective-permute-start | bytes 3145736 | tf_op jit(solution)/shard_map/ppermute | solution.py:389
  358.8 2.3 collective-permute-start.16
  358.8 3.0 collective-permute-start.20
  359.3 3.2 collective-permute-start.18
  360.5 42.1 %collective-permute-start.15 = (f32[512,256]{1,0:T(8,128)}, f32[512,256]{1,0:T(8,128)S(1)}, u32[]{:S(2)}, u32[]{:S(2)}) collective-permute-start(f32[512,256]{1,0:T(8,128)} %get-tuple-element.36), channel_id=1, source_target_pairs={{0,1},{1,0},{2,3},{3,2},{4,5},{5,4},{6,7},{7,6},{8,9},{9,8},{10,11... | collective-permute-start | bytes 1572872 | tf_op jit(solution)/shard_map/ppermute | solution.py:417
  364.6 38.0 %collective-permute-start.21 = (f32[512,256]{1,0:T(8,128)S(1)}, f32[512,256]{1,0:T(8,128)S(1)}, u32[]{:S(2)}, u32[]{:S(2)}) collective-permute-start(f32[512,256]{1,0:T(8,128)S(1)} %get-tuple-element.41), channel_id=1, source_target_pairs={{0,6},{1,7},{2,0},{3,1},{4,2},{5,3},{6,4},{7,5},{8,14},{9,15},{10,... | collective-permute-start | bytes 1572872 | tf_op jit(solution)/shard_map/ppermute | solution.py:419
  367.2 55.0 %collective-permute-start.19 = (f32[512,256]{1,0:T(8,128)S(1)}, f32[512,256]{1,0:T(8,128)S(1)}, u32[]{:S(2)}, u32[]{:S(2)}) collective-permute-start(f32[512,256]{1,0:T(8,128)S(1)} %get-tuple-element.42), channel_id=1, source_target_pairs={{0,4},{1,5},{2,6},{3,7},{4,0},{5,1},{6,2},{7,3},{8,12},{9,13},{10,... | collective-permute-start | bytes 1572872 | tf_op jit(solution)/shard_map/ppermute | solution.py:419
  399.4 24.6 %collective-permute-start.17 = (f32[512,256]{1,0:T(8,128)S(1)}, f32[512,256]{1,0:T(8,128)S(1)}, u32[]{:S(2)}, u32[]{:S(2)}) collective-permute-start(f32[512,256]{1,0:T(8,128)S(1)} %get-tuple-element.40), channel_id=1, source_target_pairs={{0,2},{1,3},{2,4},{3,5},{4,6},{5,7},{6,0},{7,1},{8,10},{9,11},{10,... | collective-permute-start | bytes 1572872 | tf_op jit(solution)/shard_map/ppermute | solution.py:419
  425.7 1.7 copy-start.4
  527.5 35.5 %copy-start.1 = (f32[512,256]{1,0:T(8,128)S(1)}, f32[512,256]{1,0:T(8,128)}, u32[]{:S(2)}) copy-start(f32[512,256]{1,0:T(8,128)} %param.6) | copy-start | bytes 1572868
